TPU v7x, 128 devices: a whole 4x4x4 slice. The times are simulated.
128 devices in a mesh: dp: 16 (over x, y), expert: 8 (over z, core).
Axes of the slice: x: 4, y: 4, z: 4, core: 2. Of those that a mesh axis runs over, the one named last changes fastest.
Arguments:
- layer_input: bfloat16 [16384, 2560], P(('dp', 'expert')), may hold values from -6 to 6
- output_grad: bfloat16 [16384, 2560], P(('dp', 'expert')), may hold values from -6 to 6
- expert_ids: int32 [16384, 2], P(('dp', 'expert')), may hold values from 0 to 7, all different within a row; in each aligned block of 128 rows (0 to 127, 128 to 255, ...) at most 48 rows name the same one
- gate_probs: bfloat16 [16384, 2], P(('dp', 'expert')), may hold values from 0.099609375 to 0.59765625
- gate_weight: float32 [8, 2560, 1536], P('expert', 'dp'), may hold values from -0.125 to 0.125
- up_weight: float32 [8, 2560, 1536], P('expert', 'dp'), may hold values from -0.125 to 0.125
- down_weight: float32 [8, 1536, 2560], P('expert', 'dp'), may hold values from -0.15625 to 0.15625
- gate_moment: float32 [8, 2560, 1536], P('expert', 'dp'), may hold values from -12 to 12
- up_moment: float32 [8, 2560, 1536], P('expert', 'dp'), may hold values from -12 to 12
- down_moment: float32 [8, 1536, 2560], P('expert', 'dp'), may hold values from -12 to 12
- gate_second: float32 [8, 2560, 1536], P('expert', 'dp'), may hold values from 1 to 100
- up_second: float32 [8, 2560, 1536], P('expert', 'dp'), may hold values from 1 to 100
- down_second: float32 [8, 1536, 2560], P('expert', 'dp'), may hold values from 1 to 100
Outputs:
- input_grad: bfloat16 [16384, 2560], P(('dp', 'expert'))
- prob_grad: bfloat16 [16384, 2], P(('dp', 'expert'))
- new_gate_weight: float32 [8, 2560, 1536], P('expert', 'dp')
- new_up_weight: float32 [8, 2560, 1536], P('expert', 'dp')
- new_down_weight: float32 [8, 1536, 2560], P('expert', 'dp')
- new_gate_moment: float32 [8, 2560, 1536], P('expert', 'dp')
- new_up_moment: float32 [8, 2560, 1536], P('expert', 'dp')
- new_down_moment: float32 [8, 1536, 2560], P('expert', 'dp')
- new_gate_second: float32 [8, 2560, 1536], P('expert', 'dp')
- new_up_second: float32 [8, 2560, 1536], P('expert', 'dp')
- new_down_second: float32 [8, 1536, 2560], P('expert', 'dp')
Inputs may be any that keep to these rules, and one draw needn't show every extreme that they name: `expert_ids`: each token names 2 different experts. Among the (token, pick) pairs of one device's 128 tokens, no expert is named more than 48 times, and in every draw some device's tokens name some expert exactly 48 times.
All inputs are finite; a program needn't handle non-finite values.
Results may differ from a plain program's by a relative error of at most 0.025.
Values may be sent and summed in bfloat16 or wider, within the bound.
No kernel may reach another device: no remote copies, remote signals or barrier semaphores. Data moves between devices by JAX's collectives and lax.ppermute only.
A program may use at most 256 MiB of HBM per device.

v0:
```python
import jax
import jax.numpy as jnp
from jax import lax
from jax.sharding import PartitionSpec as P

beta_one = 0.9
beta_two = 0.95
learn_rate = 0.003
decay_rate = 0.1
epsilon = 1e-08
correct_one = 1.0 - 2.6561398887587e-05
correct_two = 1.0 - 0.005920529220333


def slot_tables(flat_ids, expert_count, exp_dev, groups, capacity):
    onehot = (flat_ids[:, None] == jnp.arange(expert_count, dtype=jnp.int32)[None, :]).astype(
        jnp.int32
    )
    before = jnp.cumsum(onehot, axis=0) - onehot
    ranked = jnp.sum(before * onehot, axis=1)
    device = flat_ids // exp_dev
    local = flat_ids % exp_dev
    return (local * groups + device) * capacity + ranked


def adamw(weight, moment, second, grad):
    moment_new = beta_one * moment + (1.0 - beta_one) * grad
    second_new = beta_two * second + (1.0 - beta_two) * grad * grad
    update = moment_new / correct_one / (jnp.sqrt(second_new / correct_two) + epsilon)
    return (weight - learn_rate * (update + decay_rate * weight), moment_new, second_new)


def body(
    layer_input,
    output_grad,
    expert_ids,
    gate_probs,
    gate_weight,
    up_weight,
    down_weight,
    gate_moment,
    up_moment,
    down_moment,
    gate_second,
    up_second,
    down_second,
):
    exp_dev = gate_weight.shape[0]
    hidden_units = gate_weight.shape[2]
    width = layer_input.shape[1]
    groups = lax.axis_size("expert")
    shards = lax.axis_size("dp")
    tok_count, picks = expert_ids.shape
    capacity = 3 * tok_count * picks // (2 * exp_dev * groups)
    slots = exp_dev * groups * capacity
    row_count = groups * capacity
    dest_slot = slot_tables(expert_ids.reshape(-1), exp_dev * groups, exp_dev, groups, capacity)
    owner = (
        jnp.zeros((slots,), jnp.int32)
        .at[dest_slot]
        .set(jnp.arange(tok_count * picks, dtype=jnp.int32) // picks)
    )
    filled = jnp.zeros((slots,), jnp.int32).at[dest_slot].set(1) > 0
    zero_val = jnp.zeros((), jnp.bfloat16)
    send_input = jnp.where(filled[:, None], layer_input[owner], zero_val).reshape(
        exp_dev, groups, capacity, width
    )
    send_grad = jnp.where(filled[:, None], output_grad[owner], zero_val).reshape(
        exp_dev, groups, capacity, width
    )
    send_gate = (
        jnp.zeros((slots,), jnp.bfloat16)
        .at[dest_slot]
        .set(gate_probs.reshape(-1))
        .reshape(exp_dev, groups, capacity)
    )
    w_gate_up_shard = jnp.concatenate((gate_weight, up_weight), axis=2).astype(jnp.bfloat16)
    w_down_shard = down_weight.astype(jnp.bfloat16)
    w_gate_up, w_down = (
        lax.all_gather(w_gate_up_shard, "dp", axis=1, tiled=True),
        lax.all_gather(w_down_shard, "dp", axis=1, tiled=True),
    )
    recv_input, recv_grad, recv_gate = (
        lax.all_to_all(send_input, "expert", split_axis=1, concat_axis=1, tiled=True),
        lax.all_to_all(send_grad, "expert", split_axis=1, concat_axis=1, tiled=True),
        lax.all_to_all(send_gate, "expert", split_axis=1, concat_axis=1, tiled=True),
    )
    x_rows = recv_input.reshape(exp_dev, row_count, width)
    dy_rows = recv_grad.reshape(exp_dev, row_count, width)
    gate_rows = recv_gate.reshape(exp_dev, row_count)
    pre = jnp.einsum("erd,edf->erf", x_rows, w_gate_up, preferred_element_type=jnp.float32)
    gate_pre = pre[:, :, :hidden_units]
    up_pre = pre[:, :, hidden_units:]
    sigmoid_gate = jax.nn.sigmoid(gate_pre)
    silu_gate = gate_pre * sigmoid_gate
    hidden = (silu_gate * up_pre).astype(jnp.bfloat16)
    expert_out = jnp.einsum("erf,efd->erd", hidden, w_down, preferred_element_type=jnp.float32)
    prob_rows = jnp.sum(dy_rows.astype(jnp.float32) * expert_out, axis=2).astype(jnp.bfloat16)
    out_scaled = (gate_rows.astype(jnp.float32)[:, :, None] * dy_rows.astype(jnp.float32)).astype(
        jnp.bfloat16
    )
    down_cols = hidden_units // shards
    model_cols = width // shards
    hidden_grad = jnp.einsum("erd,efd->erf", out_scaled, w_down, preferred_element_type=jnp.float32)
    dsilu = sigmoid_gate * (1.0 + gate_pre * (1.0 - sigmoid_gate))
    pre_grad = jnp.concatenate(
        (hidden_grad * up_pre * dsilu, hidden_grad * silu_gate), axis=2
    ).astype(jnp.bfloat16)
    input_rows = jnp.einsum(
        "erf,edf->erd", pre_grad, w_gate_up, preferred_element_type=jnp.float32
    ).astype(jnp.bfloat16)
    cols = x_rows
    first = jnp.einsum("erc,erf->cef", cols, pre_grad, preferred_element_type=jnp.float32).reshape(
        1 * lax.axis_size("dp"), model_cols * exp_dev * 2 * hidden_units
    )
    cols = hidden
    second = jnp.einsum(
        "erc,erd->ced", cols, out_scaled, preferred_element_type=jnp.float32
    ).reshape(1 * lax.axis_size("dp"), down_cols * exp_dev * width)
    joined = lax.psum_scatter(
        jnp.concatenate((first, second), axis=1).astype(jnp.bfloat16),
        "dp",
        scatter_dimension=0,
        tiled=True,
    ).astype(jnp.float32)
    split_at = model_cols * exp_dev * 2 * hidden_units
    grad_gate_up = joined[0, :split_at].reshape(model_cols, exp_dev, 2 * hidden_units)
    grad_down = joined[0, split_at:].reshape(down_cols, exp_dev, width)
    back_input, back_prob = (
        lax.all_to_all(
            input_rows.reshape(exp_dev, groups, capacity, width),
            "expert",
            split_axis=1,
            concat_axis=1,
            tiled=True,
        ),
        lax.all_to_all(
            prob_rows.reshape(exp_dev, groups, capacity),
            "expert",
            split_axis=1,
            concat_axis=1,
            tiled=True,
        ),
    )
    picked_rows = back_input.reshape(slots, width)[dest_slot].reshape(tok_count, picks, width)
    input_grad = jnp.sum(picked_rows.astype(jnp.float32), axis=1).astype(jnp.bfloat16)
    prob_grad = back_prob.reshape(slots)[dest_slot].reshape(tok_count, picks)
    grad_gate_up = jnp.transpose(grad_gate_up, (1, 0, 2))
    grad_down = jnp.transpose(grad_down, (1, 0, 2))
    new_gate_weight, new_gate_moment, new_gate_second = adamw(
        gate_weight, gate_moment, gate_second, grad_gate_up[:, :, :hidden_units]
    )
    new_up_weight, new_up_moment, new_up_second = adamw(
        up_weight, up_moment, up_second, grad_gate_up[:, :, hidden_units:]
    )
    new_down_weight, new_down_moment, new_down_second = adamw(
        down_weight, down_moment, down_second, grad_down
    )
    return (
        input_grad,
        prob_grad,
        new_gate_weight,
        new_up_weight,
        new_down_weight,
        new_gate_moment,
        new_up_moment,
        new_down_moment,
        new_gate_second,
        new_up_second,
        new_down_second,
    )


def solution(mesh):
    return jax.shard_map(
        body,
        mesh=mesh,
        in_specs=(
            P(("dp", "expert"), None),
            P(("dp", "expert"), None),
            P(("dp", "expert"), None),
            P(("dp", "expert"), None),
            P("expert", "dp", None),
            P("expert", "dp", None),
            P("expert", "dp", None),
            P("expert", "dp", None),
            P("expert", "dp", None),
            P("expert", "dp", None),
            P("expert", "dp", None),
            P("expert", "dp", None),
            P("expert", "dp", None),
        ),
        out_specs=(
            P(("dp", "expert"), None),
            P(("dp", "expert"), None),
            P("expert", "dp", None),
            P("expert", "dp", None),
            P("expert", "dp", None),
            P("expert", "dp", None),
            P("expert", "dp", None),
            P("expert", "dp", None),
            P("expert", "dp", None),
            P("expert", "dp", None),
            P("expert", "dp", None),
        ),
        check_vma=False,
    )
```

profile of v0, /device:TPU:1, one launch (start us, length us, event | category | flops | bytes accessed | tf_op | source)
XLA Modules:
  0.0 654.3 jit_solution(8457311708946021603)
XLA Ops:
  16.7 6.8 %all-to-all-start = ((bf16[1,8,48]{2,0,1:T(2,128)(2,1)}), bf16[1,8,48]{2,0,1:T(2,128)(2,1)S(1)}, u32[]{:S(2)}, u32[]{:S(2)}) async-start(bf16[1,8,48]{2,0,1:T(2,128)(2,1)} %reshape.417), calls=%async_computation | async-start | bytes 8192 | tf_op jit(solution)/shard_map/all_to_all | solution.py:86
  36.3 30.1 %all_to_all.25 = bf16[1,8,48,2560]{3,2,0,1:T(8,128)(2,1)S(1)} all-to-all(bf16[1,8,48,2560]{3,2,0,1:T(8,128)(2,1)} %get-tuple-element.60), channel_id=1, replica_groups=mesh['dp'=16,'expert'=8] {'expert'}, dimensions={1} | all-to-all | bytes 3932160 | tf_op jit(solution)/shard_map/all_to_all | solution.py:85
  66.3 5.1 all-to-all-start.2
  74.1 22.3 %all-to-all-done.2 = bf16[1,8,48,2560]{3,2,0,1:T(8,128)(2,1)} async-done(((bf16[1,8,48,2560]{3,2,0,1:T(8,128)(2,1)}), bf16[1,8,48,2560]{3,2,0,1:T(8,128)(2,1)}, u32[]{:S(2)}, u32[]{:S(2)}) %all-to-all-start.2) | async-done | bytes 1966112 | tf_op jit(solution)/shard_map/all_to_all | solution.py:84
  96.4 23.7 %all-gather.5.cloned.1.call-done = bf16[1,2560,3072]{2,1,0:T(8,128)(2,1)} async-done(((bf16[1,160,3072]{2,1,0:T(8,128)(2,1)}), bf16[1,2560,3072]{2,1,0:T(8,128)(2,1)}) %all-gather.5.cloned.1.call-update) | async-done | bytes 15728656 | tf_op jit(solution)/shard_map/all_gather | solution.py:80
  120.2 11.7 %fusion.13 = f32[1,384,3072]{2,1,0:T(8,128)} fusion(bf16[384,2560]{1,0:T(8,128)(2,1)} %bitcast.12, bf16[1,2560,3072]{2,1,0:T(8,128)(2,1)} %all-gather.5.cloned.1.call-done), kind=kOutput, calls=%fused_computation.21 | convolution fusion | flops 6039797760 | bytes 22413312 | tf_op jit(solution)/shard_map/erd,edf->erf/dot_general | solution.py:91
  131.8 59.3 %all-gather.3.cloned.1.call-done = bf16[1,1536,2560]{2,1,0:T(8,128)(2,1)} async-done(((bf16[1,96,2560]{2,1,0:T(8,128)(2,1)}), bf16[1,1536,2560]{2,1,0:T(8,128)(2,1)}) %all-gather.3.cloned.1.call-update) | async-done | bytes 7864336 | tf_op jit(solution)/shard_map/all_gather | solution.py:81
  191.1 10.8 %fusion.29 = (bf16[384,1536]{1,0:T(8,128)(2,1)S(1)}, bf16[384,1536]{1,0:T(8,128)(2,1)}, bf16[384,1536]{1,0:T(8,128)(2,1)S(1)}) fusion(f32[1,384,3072]{2,1,0:T(8,128)} %fusion.13, bf16[1,1536,2560]{2,1,0:T(8,128)(2,1)} %all-gather.3.cloned.1.call-done, f32[1,384,1,1,1,1,2560]{6,1,5,4,3,2,0:T(8,128)} %bitcast.83, f32[384]{0:T(512)S(1)} %reshape.356), kind=kOutput, calls=%fused_computation.42 | convolution fusion | flops 3030712320 | bytes 20055552 | tf_op jit(solution)/shard_map/erd,efd->erf/dot_general | solution.py:104
  201.9 6.6 %fusion.5 = bf16[1536,1,2560]{0,2,1:T(8,128)(2,1)} fusion(bf16[384,1536]{1,0:T(8,128)(2,1)S(1)} %get-tuple-element.55, f32[1,384,1,1,1,1,2560]{6,1,5,4,3,2,0:T(8,128)S(1)} %bitcast.85, f32[384]{0:T(512)S(1)} %reshape.356), kind=kOutput, calls=%fused_computation.15 | convolution fusion | flops 3025797120 | bytes 12977664 | tf_op jit(solution)/shard_map/erc,erd->ced/dot_general | solution.py:117
  208.6 10.6 %copy.51 = bf16[1536,1,2560]{2,0,1:T(8,128)(2,1)} copy(bf16[1536,1,2560]{0,2,1:T(8,128)(2,1)} %fusion.5) | data formatting | bytes 15728640 | tf_op jit(solution)/shard_map/erc,erd->ced/transpose | solution.py:117
  219.2 7.6 %reshape.355 = bf16[16,245760]{1,0:T(8,128)(2,1)} reshape(bf16[1536,1,2560]{2,0,1:T(8,128)(2,1)} %copy.51) | data formatting | bytes 15728640 | tf_op jit(solution)/shard_map/reshape | solution.py:119
  226.8 13.6 %fusion.4 = bf16[2560,1,3072]{0,2,1:T(8,128)(2,1)} fusion(bf16[384,2560]{1,0:T(8,128)(2,1)} %bitcast.12, bf16[384,1536]{1,0:T(8,128)(2,1)} %get-tuple-element.54, bf16[384,1536]{1,0:T(8,128)(2,1)S(1)} %get-tuple-element.53), kind=kOutput, calls=%fused_computation.13 | convolution fusion | flops 6052380672 | bytes 20054016 | tf_op jit(solution)/shard_map/erc,erf->cef/dot_general | solution.py:113
  240.4 20.7 %copy.50 = bf16[2560,1,3072]{2,0,1:T(8,128)(2,1)} copy(bf16[2560,1,3072]{0,2,1:T(8,128)(2,1)} %fusion.4) | data formatting | bytes 31457280 | tf_op jit(solution)/shard_map/erc,erf->cef/transpose | solution.py:113
  261.1 19.9 %reshape.354 = bf16[16,491520]{1,0:T(8,128)(2,1)} reshape(bf16[2560,1,3072]{2,0,1:T(8,128)(2,1)} %copy.50) | data formatting | bytes 31457280 | tf_op jit(solution)/shard_map/reshape | solution.py:113
  280.9 25.0 %pad_maximum_fusion = bf16[16,737280]{1,0:T(8,128)(2,1)} fusion(bf16[16,245760]{1,0:T(8,128)(2,1)} %reshape.355, bf16[16,491520]{1,0:T(8,128)(2,1)} %reshape.354), kind=kLoop, calls=%fused_computation.7 | loop fusion | flops 47185920 | bytes 47185920 | tf_op jit(solution)/shard_map/concatenate | solution.py:121
  306.0 7.6 %fusion.24 = bf16[384]{0:T(512)(128)(2,1)S(1)} fusion(f32[384,2560]{1,0:T(8,128)} %bitcast.84, bf16[384,1536]{1,0:T(8,128)(2,1)S(1)} %get-tuple-element.55, bf16[1,1536,2560]{2,1,0:T(8,128)(2,1)} %all-gather.3.cloned.1.call-done), kind=kOutput, calls=%fused_computation.36 | convolution fusion | flops 3021864448 | bytes 12976896 | tf_op jit(solution)/shard_map/erf,efd->erd/dot_general | solution.py:97
  314.3 5.1 all-to-all-start.4
  319.4 11.2 %fusion.16 = bf16[384,2560]{1,0:T(8,128)(2,1)} fusion(bf16[1,2560,3072]{2,1,0:T(8,128)(2,1)} %all-gather.5.cloned.1.call-done, bf16[384,1536]{1,0:T(8,128)(2,1)} %get-tuple-element.54, bf16[384,1536]{1,0:T(8,128)(2,1)S(1)} %get-tuple-element.53), kind=kOutput, calls=%fused_computation.22 | convolution fusion | flops 6045499392 | bytes 20054016 | tf_op jit(solution)/shard_map/erf,edf->erd/dot_general | solution.py:109
  330.6 5.4 all-to-all-start.3
  339.4 21.5 %all-to-all-done.3 = bf16[1,8,48,2560]{3,2,0,1:T(8,128)(2,1)S(1)} async-done(((bf16[1,8,48,2560]{3,2,0,1:T(8,128)(2,1)}), bf16[1,8,48,2560]{3,2,0,1:T(8,128)(2,1)S(1)}, u32[]{:S(2)}, u32[]{:S(2)}) %all-to-all-start.3) | async-done | bytes 1966112 | tf_op jit(solution)/shard_map/all_to_all | solution.py:130
  370.9 224.2 %all-reduce.3.cloned.1.call-done = bf16[16,737280]{1,0:T(8,128)(2,1)} async-done(((bf16[16,737280]{1,0:T(8,128)(2,1)}), bf16[16,737280]{1,0:T(8,128)(2,1)}) %all-reduce.3.cloned.1.call-update) | async-done | bytes 23592976
  595.1 7.3 %dynamic-slice_convert_fusion = f32[1,737280]{1,0:T(1,128)S(1)} fusion(bf16[16,737280]{1,0:T(8,128)(2,1)} %all-reduce.3.cloned.1.call-done, u32[]{:T(128)} %bitcast.32), kind=kLoop, calls=%fused_computation.25 | loop fusion | flops 737280 | bytes 4423684 | tf_op jit(solution)/shard_map/convert_element_type | solution.py:125
  602.4 21.6 %slice_reduce_fusion = f32[491520]{0:T(1024)} fusion(f32[1,737280]{1,0:T(1,128)S(1)} %dynamic-slice_convert_fusion), kind=kLoop, calls=%fused_computation.33 | loop fusion | bytes 3932160 | tf_op jit(solution)/shard_map/slice | solution.py:127
  624.0 11.3 %slice_reduce_fusion.1 = f32[245760]{0:T(1024)} fusion(f32[1,737280]{1,0:T(1,128)S(1)} %dynamic-slice_convert_fusion), kind=kLoop, calls=%fused_computation.46 | loop fusion | bytes 1966080 | tf_op jit(solution)/shard_map/slice | solution.py:128
  (86 shorter events, 51.2 us)
Async XLA Ops:
  7.2 19.3 %copy-start = (bf16[128,2560]{1,0:T(8,128)(2,1)S(1)}, bf16[128,2560]{1,0:T(8,128)(2,1)}, u32[]{:S(2)}) copy-start(bf16[128,2560]{1,0:T(8,128)(2,1)} %param.13) | copy-start | bytes 1966084
  7.2 113.0 %all-gather.5.cloned.1.call-start = ((), (), s32[]{:S(2)}) async-start(), calls=%async_computation.6 | async-start | bytes 16711680 | tf_op jit(solution)/shard_map/all_gather | solution.py:80
  8.6 2.5 copy-start.4
  9.9 2.0 copy-start.11
  9.9 3.5 copy-start.12
  11.0 180.1 %all-gather.3.cloned.1.call-start = ((), (), s32[]{:S(2)}) async-start(), calls=%async_computation.5 | async-start | bytes 8355840 | tf_op jit(solution)/shard_map/all_gather | solution.py:81
  16.7 19.6 %all-to-all-start = ((bf16[1,8,48]{2,0,1:T(2,128)(2,1)}), bf16[1,8,48]{2,0,1:T(2,128)(2,1)S(1)}, u32[]{:S(2)}, u32[]{:S(2)}) async-start(bf16[1,8,48]{2,0,1:T(2,128)(2,1)} %reshape.417), calls=%async_computation | async-start | bytes 8192 | tf_op jit(solution)/shard_map/all_to_all | solution.py:86
  26.5 2.6 copy-start.2
  66.3 30.1 %all-to-all-start.2 = ((bf16[1,8,48,2560]{3,2,0,1:T(8,128)(2,1)}), bf16[1,8,48,2560]{3,2,0,1:T(8,128)(2,1)}, u32[]{:S(2)}, u32[]{:S(2)}) async-start(bf16[1,8,48,2560]{3,2,0,1:T(8,128)(2,1)} %get-tuple-element.59), calls=%async_computation.2 | async-start | bytes 3932160 | tf_op jit(solution)/shard_map/all_to_all | solution.py:84
  71.4 523.7 %all-reduce.3.cloned.1.call-start = ((), (), s32[]{:S(2)}) async-start(), calls=%async_computation.7 | async-start | bytes 47185920
  191.1 10.8 %copy-start.3 = (f32[1,8,48,2560]{3,2,0,1:T(8,128)S(1)}, f32[1,8,48,2560]{3,2,0,1:T(8,128)}, u32[]{:S(2)}) copy-start(f32[1,8,48,2560]{3,2,0,1:T(8,128)} %convert_element_type.140) | copy-start | bytes 11796484
  314.3 16.3 %all-to-all-start.4 = ((bf16[1,8,48]{2,0,1:T(2,128)(2,1)}), bf16[1,8,48]{2,0,1:T(2,128)(2,1)S(1)}, u32[]{:S(2)}, u32[]{:S(2)}) async-start(bf16[1,8,48]{2,0,1:T(2,128)(2,1)} %convert_element_type.142), calls=%async_computation.4 | async-start | bytes 8192 | tf_op jit(solution)/shard_map/all_to_all | solution.py:137
  330.6 5.4 copy-start.13
  330.6 30.2 %all-to-all-start.3 = ((bf16[1,8,48,2560]{3,2,0,1:T(8,128)(2,1)}), bf16[1,8,48,2560]{3,2,0,1:T(8,128)(2,1)S(1)}, u32[]{:S(2)}, u32[]{:S(2)}) async-start(bf16[1,8,48,2560]{3,2,0,1:T(8,128)(2,1)} %bitcast.86), calls=%async_computation.3 | async-start | bytes 3932160 | tf_op jit(solution)/shard_map/all_to_all | solution.py:130
  639.2 4.4 copy-start.5
  639.2 4.4 copy-start.6
  639.2 4.4 copy-start.7
  639.2 4.4 copy-start.8
  639.2 4.4 copy-start.9
  639.2 4.7 copy-start.10
  643.9 3.7 copy-start.1
Sparse Core Ops, SparseCore 0:
  11.1 108.9 all-gather.4
  122.9 68.1 all-gather.2
  306.1 288.8 all-reduce.2
where the time goes:
time: 662 us; the launch traced here: 654 us
  waiting for transfers between devices  351 us (53%)
  local copies, waits for them, and re-layouts  119 us (18%)
  matrix products  61.5 us (9%)
  other arithmetic  56.3 us (9%)
  blocking collectives  30.1 us (5%)
  starting transfers between devices  22.6 us (3%)
  between operations  14.2 us (2%)
    unnamed x4, waiting for transfers between devices  224 us
    all_gather x1, waiting for transfers between devices, body(): lax.all_gather(w_down_shard, 'dp', axis=1, tiled=True)  59.3 us
    all_to_all x1, blocking collectives, body(): lax.all_to_all(send_grad, 'expert', split_axis=1, concat_axis=1, tiled=True)  30.1 us
    concatenate x1, other arithmetic, body(): jnp.concatenate((first, second), axis=1).astype(jnp.bfloat16)  25 us
    all_gather x1, waiting for transfers between devices, body(): lax.all_gather(w_gate_up_shard, 'dp', axis=1, tiled=True)  23.7 us
    all_to_all x1, waiting for transfers between devices, body(): lax.all_to_all(send_input, 'expert', split_axis=1, concat_axis=1, tiled=T...  22.3 us
    slice x1, local copies, waits for them, and re-layouts, body(): joined[0, :split_at].reshape(model_cols, exp_dev, 2 * hidden_units)  21.6 us
    all_to_all x1, waiting for transfers between devices, body(): lax.all_to_all(input_rows.reshape(exp_dev, groups, capacity, width), 'exp...  21.5 us
  transfers between devices with their start and end apart: 7, of which 5 were waited for; matrix products, arithmetic and copies ran while one was open for 10% of the time, Pallas kernels for 0%

commit v1 on v0

--- a/solution.py
+++ b/solution.py
@@ -2,6 +2,7 @@
 import jax.numpy as jnp
 from jax import lax
 from jax.sharding import PartitionSpec as P
+from jax.lax import all_to_all, psum
 
 beta_one = 0.9
 beta_two = 0.95
@@ -76,9 +77,15 @@
     )
     w_gate_up_shard = jnp.concatenate((gate_weight, up_weight), axis=2).astype(jnp.bfloat16)
     w_down_shard = down_weight.astype(jnp.bfloat16)
+
+    def _manage_task(content):
+        back = psum(1, "dp")
+        z1 = all_to_all(jnp.stack(back * [content], 0), "dp", 0, 0)
+        return jnp.concatenate(z1, 1)
+
     w_gate_up, w_down = (
         lax.all_gather(w_gate_up_shard, "dp", axis=1, tiled=True),
-        lax.all_gather(w_down_shard, "dp", axis=1, tiled=True),
+        _manage_task(w_down_shard),
     )
     recv_input, recv_grad, recv_gate = (
         lax.all_to_all(send_input, "expert", split_axis=1, concat_axis=1, tiled=True),

time: 662 us -> 735 us (1.11)
  waiting for transfers between devices: 351 us -> 404 us
  starting transfers between devices: 22.6 us -> 34.6 us
    all_to_all x1 -> x2, waiting for transfers between devices: 22.3 us -> 91.9 us  [the longest x1 68.2 us: _manage_task(): z1 = all_to_all(jnp.stack(back * [content], 0), 'dp', 0, 0)]
    all_gather x1 -> x0, waiting for transfers between devices: 59.3 us -> none  [body(): lax.all_gather(w_down_shard, 'dp', axis=1, tiled=True)]
    all_gather x1, waiting for transfers between devices: 23.7 us -> 63.4 us  [body(): lax.all_gather(w_gate_up_shard, 'dp', axis=1, tiled=True)]
    unnamed x4 -> x3, waiting for transfers between devices: 224 us -> 228 us
where the time goes in v1:
time: 735 us; the launch traced here: 727 us
  waiting for transfers between devices  404 us (55%)
  local copies, waits for them, and re-layouts  125 us (17%)
  matrix products  62.2 us (8%)
  other arithmetic  56.6 us (8%)
  starting transfers between devices  34.6 us (5%)
  blocking collectives  29.9 us (4%)
  between operations  14.5 us (2%)
    unnamed x3, waiting for transfers between devices  228 us
    all_to_all x1, waiting for transfers between devices, _manage_task(): z1 = all_to_all(jnp.stack(back * [content], 0), 'dp', 0, 0)  68.2 us
    all_gather x1, waiting for transfers between devices, body(): lax.all_gather(w_gate_up_shard, 'dp', axis=1, tiled=True)  63.4 us
    all_to_all x1, blocking collectives, body(): lax.all_to_all(send_input, 'expert', split_axis=1, concat_axis=1, tiled=T...  29.9 us
    concatenate x1, other arithmetic, body(): jnp.concatenate((first, second), axis=1).astype(jnp.bfloat16)  25 us
    all_to_all x1, waiting for transfers between devices, body(): lax.all_to_all(send_grad, 'expert', split_axis=1, concat_axis=1, tiled=True)  23.7 us
    slice x1, local copies, waits for them, and re-layouts, body(): joined[0, :split_at].reshape(model_cols, exp_dev, 2 * hidden_units)  21.6 us
    all_to_all x1, waiting for transfers between devices, body(): lax.all_to_all(input_rows.reshape(exp_dev, groups, capacity, width), 'exp...  21.5 us
  transfers between devices with their start and end apart: 7, of which 5 were waited for; matrix products, arithmetic and copies ran while one was open for 10% of the time, Pallas kernels for 0%

profile of v1, /device:TPU:1, one launch (start us, length us, event | category | flops | bytes accessed | tf_op | source)
XLA Modules:
  0.0 727.4 jit_solution(16315947534851937295)
XLA Ops:
  15.7 6.8 all-to-all-start
  35.9 29.9 %all_to_all.30 = bf16[1,8,48,2560]{3,2,0,1:T(8,128)(2,1)} all-to-all(bf16[1,8,48,2560]{3,2,0,1:T(8,128)(2,1)S(1)} %get-tuple-element.59), channel_id=1, replica_groups=mesh['dp'=16,'expert'=8] {'expert'}, dimensions={1} | all-to-all | bytes 3932160 | tf_op jit(solution)/shard_map/all_to_all | solution.py:91
  71.4 23.7 %all-to-all-done.1 = bf16[1,8,48,2560]{3,2,0,1:T(8,128)(2,1)S(1)} async-done(((bf16[1,8,48,2560]{3,2,0,1:T(8,128)(2,1)}), bf16[1,8,48,2560]{3,2,0,1:T(8,128)(2,1)S(1)}, u32[]{:S(2)}, u32[]{:S(2)}) %all-to-all-start.1) | async-done | bytes 1966112 | tf_op jit(solution)/shard_map/all_to_all | solution.py:92
  98.9 6.8 all-to-all-start.2
  108.4 63.4 %all-gather.2.cloned.1.call-done = bf16[1,2560,3072]{2,1,0:T(8,128)(2,1)} async-done(((bf16[1,160,3072]{2,1,0:T(8,128)(2,1)}), bf16[1,2560,3072]{2,1,0:T(8,128)(2,1)}) %all-gather.2.cloned.1.call-update) | async-done | bytes 15728656 | tf_op jit(solution)/shard_map/all_gather | solution.py:87
  171.8 11.6 %fusion.6 = f32[1,384,3072]{2,1,0:T(8,128)} fusion(bf16[384,2560]{1,0:T(8,128)(2,1)} %bitcast.78, bf16[1,2560,3072]{2,1,0:T(8,128)(2,1)} %all-gather.2.cloned.1.call-done), kind=kOutput, calls=%fused_computation.17 | convolution fusion | flops 6039797760 | bytes 22413312 | tf_op jit(solution)/shard_map/erd,edf->erf/dot_general | solution.py:98
  183.4 68.2 %all-to-all-done.2 = bf16[16,1,96,2560]{3,2,1,0:T(8,128)(2,1)} async-done(((bf16[16,1,96,2560]{3,2,1,0:T(8,128)(2,1)}), bf16[16,1,96,2560]{3,2,1,0:T(8,128)(2,1)}, u32[]{:S(2)}, u32[]{:S(2)}) %all-to-all-start.2) | async-done | bytes 7864352 | tf_op jit(solution)/shard_map/all_to_all | solution.py:83
  251.6 11.2 %fusion.17 = (bf16[384,1536]{1,0:T(8,128)(2,1)}, bf16[384,1536]{1,0:T(8,128)(2,1)}, bf16[384,1536]{1,0:T(8,128)(2,1)S(1)}) fusion(f32[1,384,3072]{2,1,0:T(8,128)} %fusion.6, bf16[1536,2560]{1,0:T(8,128)(2,1)} %bitcast.9, f32[1,384,1,1,1,1,2560]{6,1,5,4,3,2,0:T(8,128)} %bitcast.75, f32[384]{0:T(512)S(1)} %reshape.362), kind=kOutput, calls=%fused_computation.38 | convolution fusion | flops 3030712320 | bytes 20055552 | tf_op jit(solution)/shard_map/erd,efd->erf/dot_general | solution.py:111
  263.9 6.7 fusion.5
  270.5 10.4 %copy.51 = bf16[1536,1,2560]{2,0,1:T(8,128)(2,1)} copy(bf16[1536,1,2560]{0,2,1:T(8,128)(2,1)} %fusion.5) | data formatting | bytes 15728640 | tf_op jit(solution)/shard_map/erc,erd->ced/transpose | solution.py:124
  281.0 7.8 %reshape.361 = bf16[16,245760]{1,0:T(8,128)(2,1)} reshape(bf16[1536,1,2560]{2,0,1:T(8,128)(2,1)} %copy.51) | data formatting | bytes 15728640 | tf_op jit(solution)/shard_map/reshape | solution.py:126
  288.7 13.7 %fusion.4 = bf16[2560,1,3072]{0,2,1:T(8,128)(2,1)} fusion(bf16[384,2560]{1,0:T(8,128)(2,1)S(1)} %bitcast.79, bf16[384,1536]{1,0:T(8,128)(2,1)} %get-tuple-element.54, bf16[384,1536]{1,0:T(8,128)(2,1)} %get-tuple-element.53), kind=kOutput, calls=%fused_computation.13 | convolution fusion | flops 6052380672 | bytes 20054016 | tf_op jit(solution)/shard_map/erc,erf->cef/dot_general | solution.py:120
  302.4 20.7 %copy.50 = bf16[2560,1,3072]{2,0,1:T(8,128)(2,1)} copy(bf16[2560,1,3072]{0,2,1:T(8,128)(2,1)} %fusion.4) | data formatting | bytes 31457280 | tf_op jit(solution)/shard_map/erc,erf->cef/transpose | solution.py:120
  323.1 19.9 %reshape.360 = bf16[16,491520]{1,0:T(8,128)(2,1)} reshape(bf16[2560,1,3072]{2,0,1:T(8,128)(2,1)} %copy.50) | data formatting | bytes 31457280 | tf_op jit(solution)/shard_map/reshape | solution.py:120
  343.0 25.0 %pad_maximum_fusion = bf16[16,737280]{1,0:T(8,128)(2,1)} fusion(bf16[16,245760]{1,0:T(8,128)(2,1)} %reshape.361, bf16[16,491520]{1,0:T(8,128)(2,1)} %reshape.360), kind=kLoop, calls=%fused_computation.7 | loop fusion | flops 47185920 | bytes 47185920 | tf_op jit(solution)/shard_map/concatenate | solution.py:128
  369.3 7.6 %fusion.14 = bf16[384]{0:T(512)(128)(2,1)S(1)} fusion(f32[384,2560]{1,0:T(8,128)} %bitcast.76, bf16[384,1536]{1,0:T(8,128)(2,1)S(1)} %copy-done.15, bf16[1536,2560]{1,0:T(8,128)(2,1)} %bitcast.9), kind=kOutput, calls=%fused_computation.32 | convolution fusion | flops 3021864448 | bytes 12976896 | tf_op jit(solution)/shard_map/erf,efd->erd/dot_general | solution.py:104
  377.6 11.0 %all-to-all-start.5 = ((bf16[1,8,48]{2,0,1:T(2,128)(2,1)}), bf16[1,8,48]{2,0,1:T(2,128)(2,1)S(1)}, u32[]{:S(2)}, u32[]{:S(2)}) async-start(bf16[1,8,48]{2,0,1:T(2,128)(2,1)} %convert_element_type.145), calls=%async_computation.5 | async-start | bytes 8192 | tf_op jit(solution)/shard_map/all_to_all | solution.py:144
  388.6 11.4 %fusion.9 = bf16[384,2560]{1,0:T(8,128)(2,1)} fusion(bf16[1,2560,3072]{2,1,0:T(8,128)(2,1)} %all-gather.2.cloned.1.call-done, bf16[384,1536]{1,0:T(8,128)(2,1)} %get-tuple-element.54, bf16[384,1536]{1,0:T(8,128)(2,1)} %get-tuple-element.53), kind=kOutput, calls=%fused_computation.18 | convolution fusion | flops 6045499392 | bytes 20054016 | tf_op jit(solution)/shard_map/erf,edf->erd/dot_general | solution.py:116
  400.0 5.4 all-to-all-start.4
  408.8 21.5 %all-to-all-done.4 = bf16[1,8,48,2560]{3,2,0,1:T(8,128)(2,1)S(1)} async-done(((bf16[1,8,48,2560]{3,2,0,1:T(8,128)(2,1)}), bf16[1,8,48,2560]{3,2,0,1:T(8,128)(2,1)S(1)}, u32[]{:S(2)}, u32[]{:S(2)}) %all-to-all-start.4) | async-done | bytes 1966112 | tf_op jit(solution)/shard_map/all_to_all | solution.py:137
  440.3 227.6 %all-reduce.3.cloned.1.call-done = bf16[16,737280]{1,0:T(8,128)(2,1)} async-done(((bf16[16,737280]{1,0:T(8,128)(2,1)}), bf16[16,737280]{1,0:T(8,128)(2,1)}) %all-reduce.3.cloned.1.call-update) | async-done | bytes 23592976
  667.9 7.3 %dynamic-slice_convert_fusion = f32[1,737280]{1,0:T(1,128)S(1)} fusion(bf16[16,737280]{1,0:T(8,128)(2,1)} %all-reduce.3.cloned.1.call-done, u32[]{:T(128)} %bitcast.33), kind=kLoop, calls=%fused_computation.21 | loop fusion | flops 737280 | bytes 4423684 | tf_op jit(solution)/shard_map/convert_element_type | solution.py:132
  675.2 21.6 %slice_reduce_fusion = f32[491520]{0:T(1024)} fusion(f32[1,737280]{1,0:T(1,128)S(1)} %dynamic-slice_convert_fusion), kind=kLoop, calls=%fused_computation.29 | loop fusion | bytes 3932160 | tf_op jit(solution)/shard_map/slice | solution.py:134
  696.8 11.3 %slice_reduce_fusion.1 = f32[245760]{0:T(1024)} fusion(f32[1,737280]{1,0:T(1,128)S(1)} %dynamic-slice_convert_fusion), kind=kLoop, calls=%fused_computation.42 | loop fusion | bytes 1966080 | tf_op jit(solution)/shard_map/slice | solution.py:135
  (90 shorter events, 62.5 us)
Async XLA Ops:
  7.2 18.3 %copy-start = (bf16[128,2560]{1,0:T(8,128)(2,1)S(1)}, bf16[128,2560]{1,0:T(8,128)(2,1)}, u32[]{:S(2)}) copy-start(bf16[128,2560]{1,0:T(8,128)(2,1)} %param.13) | copy-start | bytes 1966084
  7.2 164.6 %all-gather.2.cloned.1.call-start = ((), (), s32[]{:S(2)}) async-start(), calls=%async_computation.6 | async-start | bytes 16711680 | tf_op jit(solution)/shard_map/all_gather | solution.py:87
  8.6 2.4 copy-start.11
  8.6 3.9 copy-start.12
  15.7 20.2 %all-to-all-start = ((bf16[1,8,48]{2,0,1:T(2,128)(2,1)}), bf16[1,8,48]{2,0,1:T(2,128)(2,1)S(1)}, u32[]{:S(2)}, u32[]{:S(2)}) async-start(bf16[1,8,48]{2,0,1:T(2,128)(2,1)} %reshape.423), calls=%async_computation | async-start | bytes 8192 | tf_op jit(solution)/shard_map/all_to_all | solution.py:93
  25.5 3.3 copy-start.2
  65.8 29.3 %all-to-all-start.1 = ((bf16[1,8,48,2560]{3,2,0,1:T(8,128)(2,1)}), bf16[1,8,48,2560]{3,2,0,1:T(8,128)(2,1)S(1)}, u32[]{:S(2)}, u32[]{:S(2)}) async-start(bf16[1,8,48,2560]{3,2,0,1:T(8,128)(2,1)} %get-tuple-element.60), calls=%async_computation.1 | async-start | bytes 3932160 | tf_op jit(solution)/shard_map/all_to_all | solution.py:92
  98.9 152.7 %all-to-all-start.2 = ((bf16[16,1,96,2560]{3,2,1,0:T(8,128)(2,1)}), bf16[16,1,96,2560]{3,2,1,0:T(8,128)(2,1)}, u32[]{:S(2)}, u32[]{:S(2)}) async-start(bf16[16,1,96,2560]{3,2,1,0:T(8,128)(2,1)} %stack.2), calls=%async_computation.2 | async-start | bytes 15728640 | tf_op jit(solution)/shard_map/all_to_all | solution.py:83
  105.7 562.1 %all-reduce.3.cloned.1.call-start = ((), (), s32[]{:S(2)}) async-start(), calls=%async_computation.7 | async-start | bytes 47185920
  251.6 12.2 %copy-start.3 = (f32[1,8,48,2560]{3,2,0,1:T(8,128)S(1)}, f32[1,8,48,2560]{3,2,0,1:T(8,128)}, u32[]{:S(2)}) copy-start(f32[1,8,48,2560]{3,2,0,1:T(8,128)} %convert_element_type.143) | copy-start | bytes 11796484
  262.8 1.0 copy-start.14
  281.0 7.8 %copy-start.6 = (bf16[1,8,48,2560]{3,2,0,1:T(8,128)(2,1)S(1)}, bf16[1,8,48,2560]{3,2,0,1:T(8,128)(2,1)}, u32[]{:S(2)}) copy-start(bf16[1,8,48,2560]{3,2,0,1:T(8,128)(2,1)} %all_to_all.30) | copy-start | bytes 5898244
  368.0 1.3 copy-start.15
  377.6 22.4 %all-to-all-start.5 = ((bf16[1,8,48]{2,0,1:T(2,128)(2,1)}), bf16[1,8,48]{2,0,1:T(2,128)(2,1)S(1)}, u32[]{:S(2)}, u32[]{:S(2)}) async-start(bf16[1,8,48]{2,0,1:T(2,128)(2,1)} %convert_element_type.145), calls=%async_computation.5 | async-start | bytes 8192 | tf_op jit(solution)/shard_map/all_to_all | solution.py:144
  400.0 5.4 copy-start.13
  400.0 30.3 %all-to-all-start.4 = ((bf16[1,8,48,2560]{3,2,0,1:T(8,128)(2,1)}), bf16[1,8,48,2560]{3,2,0,1:T(8,128)(2,1)S(1)}, u32[]{:S(2)}, u32[]{:S(2)}) async-start(bf16[1,8,48,2560]{3,2,0,1:T(8,128)(2,1)} %bitcast.80), calls=%async_computation.4 | async-start | bytes 3932160 | tf_op jit(solution)/shard_map/all_to_all | solution.py:137
  712.0 4.4 copy-start.4
  712.0 4.4 copy-start.5
  712.0 4.4 copy-start.7
  712.0 4.4 copy-start.8
  712.0 4.4 copy-start.9
  712.0 4.7 copy-start.10
  716.7 3.7 copy-start.1
Sparse Core Ops, SparseCore 0:
  11.0 160.6 all-gather.1
  368.1 299.6 all-reduce.2
